TPU v7x, 32 devices: a whole 2x2x4 slice. The times are simulated.
32 devices in a mesh: dp: 16 (over z, x, core), tensor: 2 (over y).
Axes of the slice: x: 2, y: 2, z: 4, core: 2. Of those that a mesh axis runs over, the one named last changes fastest.
Arguments:
- tokens: bfloat16 [16, 736, 1152], P('dp', 'tensor'), may hold values from -6 to 6
- cotangent: bfloat16 [16, 736, 1152], P('dp', 'tensor'), may hold values from -6 to 6
- counts: int32 [16], P('dp'), may hold values from 638 to 729
- joint_weight: float32 [1152, 3, 1152], P('dp', None, 'tensor'), may hold values from -0.1875 to 0.1875
- joint_moment: float32 [1152, 3, 1152], P('dp', None, 'tensor'), may hold values from -0.0014648438 to 0.0014648438
- joint_square: float32 [1152, 3, 1152], P('dp', None, 'tensor'), may hold values from 4.53793e-09 to 3.630344e-08
- output_weight: float32 [1152, 1152], P('tensor', 'dp'), may hold values from -0.5 to 0.5
- output_moment: float32 [1152, 1152], P('tensor', 'dp'), may hold values from -0.0029296875 to 0.0029296875
- output_square: float32 [1152, 1152], P('tensor', 'dp'), may hold values from 1.815172e-08 to 1.4521376e-07
- expand_weight: float32 [1152, 4304], P('dp', 'tensor'), may hold values from -0.1875 to 0.1875
- expand_moment: float32 [1152, 4304], P('dp', 'tensor'), may hold values from -0.0029296875 to 0.0029296875
- expand_square: float32 [1152, 4304], P('dp', 'tensor'), may hold values from 1.815172e-08 to 1.4521376e-07
- reduce_weight: float32 [4304, 1152], P('tensor', 'dp'), may hold values from -0.09375 to 0.09375
- reduce_moment: float32 [4304, 1152], P('tensor', 'dp'), may hold values from -0.005859375 to 0.005859375
- reduce_square: float32 [4304, 1152], P('tensor', 'dp'), may hold values from 7.260688e-08 to 5.8085504e-07
- norm_gains: float32 [2, 1152], replicated, may hold values from 0.5 to 1.5
- gains_moment: float32 [2, 1152], replicated, may hold values from -0.009765625 to 0.009765625
- gains_square: float32 [2, 1152], replicated, may hold values from 2.0168576e-07 to 1.6134861e-06
- shifts: float32 [4, 1152], replicated, may hold values from -3 to 3
- shifts_moment: float32 [4, 1152], replicated, may hold values from -0.009765625 to 0.009765625
- shifts_square: float32 [4, 1152], replicated, may hold values from 2.0168576e-07 to 1.6134861e-06
- head_bias: float32 [2, 1152], P(None, 'tensor'), may hold values from -3 to 3
- head_moment: float32 [2, 1152], P(None, 'tensor'), may hold values from -0.0029296875 to 0.0029296875
- head_square: float32 [2, 1152], P(None, 'tensor'), may hold values from 1.815172e-08 to 1.4521376e-07
- hidden_bias: float32 [4304], P('tensor'), may hold values from -3 to 3
- hidden_moment: float32 [4304], P('tensor'), may hold values from -0.0029296875 to 0.0029296875
- hidden_square: float32 [4304], P('tensor'), may hold values from 1.815172e-08 to 1.4521376e-07
Outputs:
- layer_out: bfloat16 [16, 736, 1152], P('dp', 'tensor')
- input_grad: bfloat16 [16, 736, 1152], P('dp', 'tensor')
- grad_norm: float32 [], replicated
- joint_new: float32 [1152, 3, 1152], P('dp', None, 'tensor')
- joint_moment_new: float32 [1152, 3, 1152], P('dp', None, 'tensor')
- joint_square_new: float32 [1152, 3, 1152], P('dp', None, 'tensor')
- joint_copy: bfloat16 [1152, 3, 1152], P('dp', None, 'tensor')
- output_new: float32 [1152, 1152], P('tensor', 'dp')
- output_moment_new: float32 [1152, 1152], P('tensor', 'dp')
- output_square_new: float32 [1152, 1152], P('tensor', 'dp')
- output_copy: bfloat16 [1152, 1152], P('tensor', 'dp')
- expand_new: float32 [1152, 4304], P('dp', 'tensor')
- expand_moment_new: float32 [1152, 4304], P('dp', 'tensor')
- expand_square_new: float32 [1152, 4304], P('dp', 'tensor')
- expand_copy: bfloat16 [1152, 4304], P('dp', 'tensor')
- reduce_new: float32 [4304, 1152], P('tensor', 'dp')
- reduce_moment_new: float32 [4304, 1152], P('tensor', 'dp')
- reduce_square_new: float32 [4304, 1152], P('tensor', 'dp')
- reduce_copy: bfloat16 [4304, 1152], P('tensor', 'dp')
- gains_new: float32 [2, 1152], replicated
- gains_moment_new: float32 [2, 1152], replicated
- gains_square_new: float32 [2, 1152], replicated
- shifts_new: float32 [4, 1152], replicated
- shifts_moment_new: float32 [4, 1152], replicated
- shifts_square_new: float32 [4, 1152], replicated
- head_new: float32 [2, 1152], P(None, 'tensor')
- head_moment_new: float32 [2, 1152], P(None, 'tensor')
- head_square_new: float32 [2, 1152], P(None, 'tensor')
- hidden_new: float32 [4304], P('tensor')
- hidden_moment_new: float32 [4304], P('tensor')
- hidden_square_new: float32 [4304], P('tensor')
Inputs may be any that keep to these rules, and one draw needn't show every extreme that they name: `counts`: valid tokens of each image; key slots from there up to 736 are padding.
All inputs are finite; a program needn't handle non-finite values.
Results may differ from a plain program's by a relative error of at most 0.01.
Values may be sent and summed in bfloat16 or wider, within the bound.
A program may use at most 192 MiB of HBM per device.

v0:
```python
import jax
import jax.numpy as jnp
from jax import lax
from jax.sharding import PartitionSpec as P

HD = 72
STEP = 4


norm_eps = 1e-06
clip_limit = 1.0
matrix_rate = 0.03
vector_rate = 0.3
decay_rate = 0.1
adam_eps = 1e-08
mask_fill = -1e30


def layer_norm(values, gain, shift):
    center = jnp.mean(values, axis=-1, keepdims=True)
    centred = values - center
    spread = jnp.mean(centred * centred, axis=-1, keepdims=True)
    return centred * lax.rsqrt(spread + norm_eps) * gain + shift


def gelu_tanh(values):
    return jax.nn.gelu(values, approximate=True)


def whole_rows(part):
    return lax.all_gather(part, "tensor", axis=1, tiled=True)


def share_rows(full):
    return lax.psum_scatter(
        full.astype(jnp.bfloat16), "tensor", scatter_dimension=1, tiled=True
    ).astype(jnp.float32)


def split_heads(joint):
    length = joint.shape[0]
    heads_local = joint.shape[2] // HD
    query = joint[:, 0].reshape(length, heads_local, HD)
    keys = joint[:, 1].reshape(length, heads_local, HD)
    values = joint[:, 2].reshape(length, heads_local, HD)
    return (query, keys, values)


def masked_scores(query, keys, count):
    length = query.shape[0]
    scores = jnp.einsum("qhd,khd->hqk", query, keys, preferred_element_type=jnp.float32) * HD ** (
        -0.5
    )
    valid = jnp.arange(length, dtype=jnp.int32) < count
    return jnp.where(valid[None, None, :], scores, mask_fill)


def attend(joint, count):
    query, keys, values = split_heads(joint)
    scores = masked_scores(query, keys, count)
    top = jnp.max(scores, axis=-1, keepdims=True)
    total = jnp.sum(jnp.exp(scores - top), axis=-1, keepdims=True)
    logsum = top + jnp.log(total)
    probs = jnp.exp(scores - logsum)
    mixed = jnp.einsum(
        "hqk,khd->qhd", probs.astype(jnp.bfloat16), values, preferred_element_type=jnp.float32
    )
    return (mixed.reshape(joint.shape[0], joint.shape[2]).astype(jnp.bfloat16), logsum[:, :, 0])


def attend_back(joint, mixed_grad, logsum, count):
    query, keys, values = split_heads(joint)
    length = joint.shape[0]
    grad_heads = mixed_grad.reshape(length, joint.shape[2] // HD, HD)
    scores = masked_scores(query, keys, count)
    probs = jnp.exp(scores - logsum[:, :, None])
    value_grad = jnp.einsum(
        "hqk,qhd->khd", probs.astype(jnp.bfloat16), grad_heads, preferred_element_type=jnp.float32
    )
    prob_grad = jnp.einsum("qhd,khd->hqk", grad_heads, values, preferred_element_type=jnp.float32)
    inner = jnp.sum(probs * prob_grad, axis=-1, keepdims=True)
    score_grad = (probs * (prob_grad - inner)).astype(jnp.bfloat16)
    query_grad = jnp.einsum(
        "hqk,khd->qhd", score_grad, keys, preferred_element_type=jnp.float32
    ) * HD ** (-0.5)
    key_grad = jnp.einsum(
        "hqk,qhd->khd", score_grad, query, preferred_element_type=jnp.float32
    ) * HD ** (-0.5)
    stacked = jnp.stack([query_grad, key_grad, value_grad], axis=1)
    return stacked.reshape(length, 3, joint.shape[2]).astype(jnp.bfloat16)


def forward_pass(tokens, counts, weights, small):
    joint_w, expand_w, output_w, reduce_w = weights
    norm_gains, shifts, head_bias, hidden_bias = small
    rows = tokens.astype(jnp.float32)
    normed, first_back = jax.vjp(layer_norm, rows, norm_gains[0], shifts[0])
    normed_whole = whole_rows(normed.astype(jnp.bfloat16))
    joint = jnp.einsum("bsd,dch->bsch", normed_whole, joint_w, preferred_element_type=jnp.float32)
    bias = jnp.stack([head_bias[0], jnp.zeros_like(head_bias[0]), head_bias[1]])
    joint = (joint + bias).astype(jnp.bfloat16)
    mixed, logsum = lax.map(lambda pair: attend(pair[0], pair[1]), (joint, counts))
    branch = (
        share_rows(jnp.einsum("bsh,hd->bsd", mixed, output_w, preferred_element_type=jnp.float32))
        + shifts[2]
    )
    middle = rows + branch
    second, second_back = jax.vjp(layer_norm, middle, norm_gains[1], shifts[1])
    second_whole = whole_rows(second.astype(jnp.bfloat16))
    before = (
        jnp.einsum("bsd,df->bsf", second_whole, expand_w, preferred_element_type=jnp.float32)
        + hidden_bias
    )
    active, gelu_back = jax.vjp(gelu_tanh, before)
    active = active.astype(jnp.bfloat16)
    result = (
        share_rows(jnp.einsum("bsf,fd->bsd", active, reduce_w, preferred_element_type=jnp.float32))
        + shifts[3]
    )
    saved = (
        first_back,
        normed_whole,
        joint,
        mixed,
        logsum,
        second_back,
        second_whole,
        active,
        gelu_back,
    )
    return (middle + result, saved)


def adamw_step(weight, grad, moment, square, factor, rate, decay):
    clipped = grad * factor
    moment_new = 0.5 * moment + 0.5 * clipped
    square_new = 0.5 * square + 0.5 * clipped * clipped
    correct = 1.0 - 0.5**STEP
    update = moment_new / correct / (jnp.sqrt(square_new / correct) + adam_eps)
    return (weight - rate * (update + decay * weight), moment_new, square_new)


def squares(values):
    return jnp.sum(values * values)


def on_device(
    tokens,
    cotangent,
    counts,
    joint_weight,
    joint_moment,
    joint_square,
    output_weight,
    output_moment,
    output_square,
    expand_weight,
    expand_moment,
    expand_square,
    reduce_weight,
    reduce_moment,
    reduce_square,
    norm_gains,
    gains_moment,
    gains_square,
    shifts,
    shifts_moment,
    shifts_square,
    head_bias,
    head_moment,
    head_square,
    hidden_bias,
    hidden_moment,
    hidden_square,
):
    first_pair = (
        lax.all_gather(joint_weight.astype(jnp.bfloat16), "dp", axis=0, tiled=True),
        lax.all_gather(expand_weight.astype(jnp.bfloat16), "dp", axis=0, tiled=True),
    )
    second_pair = (
        lax.all_gather(output_weight.astype(jnp.bfloat16), "dp", axis=1, tiled=True),
        lax.all_gather(reduce_weight.astype(jnp.bfloat16), "dp", axis=1, tiled=True),
    )
    weights = (first_pair[0], first_pair[1], second_pair[0], second_pair[1])
    small = (norm_gains, shifts, head_bias, hidden_bias)
    layer_rows, saved = forward_pass(tokens, counts, weights, small)
    layer_out = layer_rows.astype(jnp.bfloat16)
    tokens_held, counts_held, weights_held, anchor = lax.optimization_barrier(
        (tokens, counts, weights, layer_out)
    )
    unused, saved = forward_pass(tokens_held, counts_held, weights_held, small)
    first_back, normed_whole, joint, mixed, logsum, second_back, second_whole, active, gelu_back = (
        saved
    )
    joint_w, expand_w, output_w, reduce_w = weights
    grad_rows = cotangent.astype(jnp.float32)
    grad_whole = whole_rows(cotangent)
    reduce_grad = jnp.einsum("bsf,bsd->fd", active, grad_whole, preferred_element_type=jnp.float32)
    active_grad = jnp.einsum(
        "bsd,fd->bsf", grad_whole, reduce_w, preferred_element_type=jnp.float32
    )
    before_grad = gelu_back(active_grad)[0].astype(jnp.bfloat16)
    expand_grad = jnp.einsum(
        "bsd,bsf->df", second_whole, before_grad, preferred_element_type=jnp.float32
    )
    hidden_grad = jnp.sum(before_grad, axis=(0, 1), dtype=jnp.float32)
    second_grad = share_rows(
        jnp.einsum("bsf,df->bsd", before_grad, expand_w, preferred_element_type=jnp.float32)
    )
    middle_part, gain_two, shift_two = second_back(second_grad)
    middle_grad = grad_rows + middle_part
    branch_grad = middle_grad.astype(jnp.bfloat16)
    branch_whole = whole_rows(branch_grad)
    output_grad = jnp.einsum("bsh,bsd->hd", mixed, branch_whole, preferred_element_type=jnp.float32)
    mixed_grad = jnp.einsum(
        "bsd,hd->bsh", branch_whole, output_w, preferred_element_type=jnp.float32
    ).astype(jnp.bfloat16)
    joint_grad = lax.map(
        lambda group: attend_back(group[0], group[1], group[2], group[3]),
        (joint, mixed_grad, logsum, counts),
    )
    joint_weight_grad = jnp.einsum(
        "bsd,bsch->dch", normed_whole, joint_grad, preferred_element_type=jnp.float32
    )
    head_grad = jnp.sum(joint_grad[:, :, 0::2], axis=(0, 1), dtype=jnp.float32)
    first_grad = share_rows(
        jnp.einsum("bsch,dch->bsd", joint_grad, joint_w, preferred_element_type=jnp.float32)
    )
    rows_part, gain_one, shift_one = first_back(first_grad)
    input_grad = (middle_grad + rows_part).astype(jnp.bfloat16)
    gain_grad = jnp.stack([gain_one, gain_two])
    shift_grad = jnp.stack(
        [
            shift_one,
            shift_two,
            jnp.sum(branch_grad, axis=(0, 1), dtype=jnp.float32),
            jnp.sum(grad_rows, axis=(0, 1)),
        ]
    )
    joint_sum, expand_sum = (
        lax.psum_scatter(joint_weight_grad, "dp", scatter_dimension=0, tiled=True),
        lax.psum_scatter(expand_grad, "dp", scatter_dimension=0, tiled=True),
    )
    output_sum, reduce_sum = (
        lax.psum_scatter(output_grad, "dp", scatter_dimension=1, tiled=True),
        lax.psum_scatter(reduce_grad, "dp", scatter_dimension=1, tiled=True),
    )
    gain_sum, shift_sum = lax.psum((gain_grad, shift_grad), ("dp", "tensor"))
    head_sum, hidden_sum = lax.psum((head_grad, hidden_grad), "dp")
    data_count = lax.axis_size("dp")
    split_count = lax.axis_size("tensor")
    owned = squares(joint_sum) + squares(expand_sum) + squares(output_sum) + squares(reduce_sum)
    shared = (squares(head_sum) + squares(hidden_sum)) / data_count
    everywhere = (squares(gain_sum) + squares(shift_sum)) / (data_count * split_count)
    grad_norm = jnp.sqrt(lax.psum(owned + shared + everywhere, ("dp", "tensor")))
    factor = clip_limit / jnp.maximum(grad_norm, clip_limit)
    joint_state = adamw_step(
        joint_weight, joint_sum, joint_moment, joint_square, factor, matrix_rate, decay_rate
    )
    output_state = adamw_step(
        output_weight, output_sum, output_moment, output_square, factor, matrix_rate, decay_rate
    )
    expand_state = adamw_step(
        expand_weight, expand_sum, expand_moment, expand_square, factor, matrix_rate, decay_rate
    )
    reduce_state = adamw_step(
        reduce_weight, reduce_sum, reduce_moment, reduce_square, factor, matrix_rate, decay_rate
    )
    gains_state = adamw_step(
        norm_gains, gain_sum, gains_moment, gains_square, factor, vector_rate, 0.0
    )
    shifts_state = adamw_step(
        shifts, shift_sum, shifts_moment, shifts_square, factor, vector_rate, 0.0
    )
    head_state = adamw_step(head_bias, head_sum, head_moment, head_square, factor, vector_rate, 0.0)
    hidden_state = adamw_step(
        hidden_bias, hidden_sum, hidden_moment, hidden_square, factor, vector_rate, 0.0
    )
    return (
        layer_out,
        input_grad,
        grad_norm,
        joint_state[0],
        joint_state[1],
        joint_state[2],
        joint_state[0].astype(jnp.bfloat16),
        output_state[0],
        output_state[1],
        output_state[2],
        output_state[0].astype(jnp.bfloat16),
        expand_state[0],
        expand_state[1],
        expand_state[2],
        expand_state[0].astype(jnp.bfloat16),
        reduce_state[0],
        reduce_state[1],
        reduce_state[2],
        reduce_state[0].astype(jnp.bfloat16),
        gains_state[0],
        gains_state[1],
        gains_state[2],
        shifts_state[0],
        shifts_state[1],
        shifts_state[2],
        head_state[0],
        head_state[1],
        head_state[2],
        hidden_state[0],
        hidden_state[1],
        hidden_state[2],
    )


def solution(mesh):
    in_specs = (
        P("dp", "tensor", None),
        P("dp", "tensor", None),
        P("dp"),
        P("dp", None, "tensor"),
        P("dp", None, "tensor"),
        P("dp", None, "tensor"),
        P("tensor", "dp"),
        P("tensor", "dp"),
        P("tensor", "dp"),
        P("dp", "tensor"),
        P("dp", "tensor"),
        P("dp", "tensor"),
        P("tensor", "dp"),
        P("tensor", "dp"),
        P("tensor", "dp"),
        P(),
        P(),
        P(),
        P(),
        P(),
        P(),
        P(None, "tensor"),
        P(None, "tensor"),
        P(None, "tensor"),
        P("tensor"),
        P("tensor"),
        P("tensor"),
    )
    out_specs = (
        P("dp", "tensor", None),
        P("dp", "tensor", None),
        P(),
        P("dp", None, "tensor"),
        P("dp", None, "tensor"),
        P("dp", None, "tensor"),
        P("dp", None, "tensor"),
        P("tensor", "dp"),
        P("tensor", "dp"),
        P("tensor", "dp"),
        P("tensor", "dp"),
        P("dp", "tensor"),
        P("dp", "tensor"),
        P("dp", "tensor"),
        P("dp", "tensor"),
        P("tensor", "dp"),
        P("tensor", "dp"),
        P("tensor", "dp"),
        P("tensor", "dp"),
        P(),
        P(),
        P(),
        P(),
        P(),
        P(),
        P(None, "tensor"),
        P(None, "tensor"),
        P(None, "tensor"),
        P("tensor"),
        P("tensor"),
        P("tensor"),
    )
    return jax.shard_map(
        on_device, mesh=mesh, in_specs=in_specs, out_specs=out_specs, check_vma=False
    )
```

profile of v0, /device:TPU:0, one launch (start us, length us, event | category | flops | bytes accessed | tf_op | source)
XLA Modules:
  0.0 1164.4 jit_solution(15240999466270216072)
XLA Ops:
  16.1 29.0 %all-gather.11.cloned.1.call-done = bf16[1,736,1152]{2,1,0:T(8,128)(2,1)} async-done(((bf16[1,368,1152]{2,1,0:T(8,128)(2,1)}), bf16[1,736,1152]{2,1,0:T(8,128)(2,1)}) %all-gather.11.cloned.1.call-update) | async-done | bytes 1695760 | tf_op jit(solution)/shard_map/all_gather | solution.py:31
  45.1 54.5 %all-gather.13.cloned.1.call-done = bf16[1152,3,576]{2,0,1:T(8,128)(2,1)} async-done(((bf16[72,3,576]{2,0,1:T(8,128)(2,1)}), bf16[1152,3,576]{2,0,1:T(8,128)(2,1)}) %all-gather.13.cloned.1.call-update) | async-done | bytes 3981328 | tf_op jit(solution)/shard_map/all_gather | solution.py:177
  114.8 10.1 exponential_reduce_fusion.1
  124.8 8.7 fusion.79
  146.6 24.4 %reduce-scatter.16.cloned.1.call-done = bf16[1,368,1152]{2,1,0:T(8,128)(2,1)} async-done(((bf16[1,736,1152]{2,1,0:T(8,128)(2,1)}), bf16[1,368,1152]{2,1,0:T(8,128)(2,1)}) %reduce-scatter.16.cloned.1.call-update) | async-done | bytes 847888 | tf_op jit(solution)/shard_map/reduce_scatter | solution.py:35
  176.2 52.6 %all-gather.19.cloned.1.call-done = bf16[1152,2152]{1,0:T(8,128)(2,1)} async-done(((bf16[72,2152]{1,0:T(8,128)(2,1)}), bf16[1152,2152]{1,0:T(8,128)(2,1)}) %all-gather.19.cloned.1.call-update) | async-done | bytes 4958224 | tf_op jit(solution)/shard_map/all_gather | solution.py:178
  228.8 56.3 %all-gather.21.cloned.1.call-done = bf16[2152,1152]{0,1:T(8,128)(2,1)} async-done(((bf16[2152,72]{0,1:T(8,128)(2,1)}), bf16[2152,1152]{0,1:T(8,128)(2,1)}) %all-gather.21.cloned.1.call-update) | async-done | bytes 4958224 | tf_op jit(solution)/shard_map/all_gather | solution.py:182
  285.1 29.4 %all-gather.17.cloned.1.call-done = bf16[1,736,1152]{2,1,0:T(8,128)(2,1)} async-done(((bf16[1,368,1152]{2,1,0:T(8,128)(2,1)}), bf16[1,736,1152]{2,1,0:T(8,128)(2,1)}) %all-gather.17.cloned.1.call-update) | async-done | bytes 1695760 | tf_op jit(solution)/shard_map/all_gather | solution.py:31
  314.5 14.5 %fusion.35 = bf16[1,736,1152]{2,1,0:T(8,128)(2,1)} fusion(bf16[2152,1152]{0,1:T(8,128)(2,1)} %all-gather.21.cloned.1.call-done, bf16[1152,2152]{1,0:T(8,128)(2,1)} %all-gather.19.cloned.1.call-done, f32[2152]{0:T(1024)S(1)} %copy-done.45, bf16[1,736,1152]{2,1,0:T(8,128)(2,1)} %all-gather.17.cloned.1.call-done), kind=kOutput, calls=%fused_computation.56 | convolution fusion | flops 7315168768 | bytes 13316512 | tf_op jit(solution)/shard_map/bsf,fd->bsd/dot_general | solution.py:117
  329.1 27.5 %reduce-scatter.18.cloned.1.call-done = bf16[1,368,1152]{2,1,0:T(8,128)(2,1)} async-done(((bf16[1,736,1152]{2,1,0:T(8,128)(2,1)}), bf16[1,368,1152]{2,1,0:T(8,128)(2,1)}) %reduce-scatter.18.cloned.1.call-update) | async-done | bytes 847888 | tf_op jit(solution)/shard_map/reduce_scatter | solution.py:35
  361.1 28.7 %all-gather.25.cloned.1.call-done = bf16[1,736,1152]{2,1,0:T(8,128)(2,1)} async-done(((bf16[1,368,1152]{2,1,0:T(8,128)(2,1)}), bf16[1,736,1152]{2,1,0:T(8,128)(2,1)}) %all-gather.25.cloned.1.call-update) | async-done | bytes 1695760 | tf_op jit(solution)/shard_map/all_gather | solution.py:31
  405.0 10.0 exponential_reduce_fusion
  415.0 8.8 fusion.78
  426.9 27.5 %reduce-scatter.20.cloned.1.call-done = bf16[1,368,1152]{2,1,0:T(8,128)(2,1)} async-done(((bf16[1,736,1152]{2,1,0:T(8,128)(2,1)}), bf16[1,368,1152]{2,1,0:T(8,128)(2,1)}) %reduce-scatter.20.cloned.1.call-update) | async-done | bytes 847888 | tf_op jit(solution)/shard_map/reduce_scatter | solution.py:35
  459.9 27.9 %all-gather.27.cloned.1.call-done = bf16[1,736,1152]{2,1,0:T(8,128)(2,1)} async-done(((bf16[1,368,1152]{2,1,0:T(8,128)(2,1)}), bf16[1,736,1152]{2,1,0:T(8,128)(2,1)}) %all-gather.27.cloned.1.call-update) | async-done | bytes 1695760 | tf_op jit(solution)/shard_map/all_gather | solution.py:31
  487.8 10.1 fusion.64
  498.0 20.0 %all-gather.23.cloned.1.call-done = bf16[1,736,1152]{2,1,0:T(8,128)(2,1)} async-done(((bf16[1,368,1152]{2,1,0:T(8,128)(2,1)}), bf16[1,736,1152]{2,1,0:T(8,128)(2,1)}) %all-gather.23.cloned.1.call-update) | async-done | bytes 1695760 | tf_op jit(solution)/shard_map/all_gather | solution.py:31
  517.9 11.3 convert_reduce_fusion
  539.1 27.5 %reduce-scatter.22.cloned.1.call-done = bf16[1,368,1152]{2,1,0:T(8,128)(2,1)} async-done(((bf16[1,736,1152]{2,1,0:T(8,128)(2,1)}), bf16[1,368,1152]{2,1,0:T(8,128)(2,1)}) %reduce-scatter.22.cloned.1.call-update) | async-done | bytes 847888 | tf_op jit(solution)/shard_map/reduce_scatter | solution.py:35
  571.5 28.3 %all-gather.29.cloned.1.call-done = bf16[1,736,1152]{2,1,0:T(8,128)(2,1)} async-done(((bf16[1,368,1152]{2,1,0:T(8,128)(2,1)}), bf16[1,736,1152]{2,1,0:T(8,128)(2,1)}) %all-gather.29.cloned.1.call-update) | async-done | bytes 1695760 | tf_op jit(solution)/shard_map/all_gather | solution.py:31
  603.1 8.6 fusion.80
  611.7 13.1 %multiply_reduce_fusion = (f32[8,736]{1,0:T(8,128)S(1)}, f32[8,736,736]{1,2,0:T(8,128)}) fusion(f32[8,736,736]{1,2,0:T(8,128)} %get-tuple-element.148, f32[8,736]{1,0:T(8,128)S(1)} %log_add_fusion, pred[736]{0:T(1024)(128)(4,1)S(1)} %iota_compare_fusion.1, bf16[736,8,72]{0,2,1:T(8,128)(2,1)S(1)} %bitcast.134, bf16[736,8,72]{0,2,1:T(8,128)(2,1)S(1)} %bitcast.123), kind=kOutput, calls=%fused_computation.1 | convolution fusion | flops 645695744 | bytes 36412128 | tf_op jit(solution)/shard_map/while/body/eval_jaxpr/qhd,khd->hqk/dot_general | solution.py:80
  624.8 13.1 %multiply_convert_fusion = bf16[8,736,736]{1,2,0:T(8,128)(2,1)S(1)} fusion(f32[8,736,736]{1,2,0:T(8,128)} %get-tuple-element.150, f32[8,736,736]{1,2,0:T(8,128)} %get-tuple-element.148, f32[8,736]{1,0:T(8,128)S(1)} %get-tuple-element.149, f32[8,736]{1,0:T(8,128)S(1)} %log_add_fusion, pred[736]{0:T(1024)(128)(4,1)S(1)} %iota_compare_fusion.1), kind=kLoop, calls=%fused_computation | loop fusion | flops 26001408 | bytes 43383520 | tf_op jit(solution)/shard_map/while/body/eval_jaxpr/convert_element_type | solution.py:82
  654.2 12.2 %fusion.26 = f32[2152,1152]{0,1:T(8,128)} fusion(f32[736,2152]{1,0:T(8,128)} %fusion.64, f32[2152]{0:T(1024)S(1)} %copy-done.45, bf16[1,736,1152]{2,1,0:T(8,128)(2,1)} %all-gather.23.cloned.1.call-done), kind=kOutput, calls=%fused_computation.47 | convolution fusion | flops 3665079808 | bytes 17956256 | tf_op jit(solution)/shard_map/bsf,bsd->fd/dot_general | solution.py:198
  666.5 10.6 fusion.62
  677.4 9.6 fusion.66
  689.6 61.9 %all-reduce.4 = (f32[2,576]{1,0:T(2,128)S(1)}, f32[2152]{0:T(1024)S(1)}) all-reduce(f32[2,576]{1,0:T(2,128)S(1)} %convert_reduce_fusion.1, f32[2152]{0:T(1024)S(1)} %get-tuple-element.151), channel_id=1, replica_groups=mesh['dp'=16,'tensor'=2] {'dp'}, use_global_device_ids=true, to_apply=%region_31.32 | all-reduce | flops 3304 | bytes 26432 | tf_op jit(solution)/shard_map/psum | solution.py:249
  760.2 40.1 %all-reduce.3 = (f32[2,1152]{1,0:T(2,128)S(1)}, f32[4,1152]{1,0:T(4,128)S(1)}) all-reduce(f32[2,1152]{1,0:T(2,128)S(1)} %pad_maximum_fusion.6, f32[4,1152]{1,0:T(4,128)S(1)} %pad_maximum_fusion.4), channel_id=1, replica_groups=mesh['dp'=16,'tensor'=2] {'dp','tensor'}, use_global_device_ids=true, to_apply=%region_38.39 | all-reduce | flops 6912 | bytes 55296 | tf_op jit(solution)/shard_map/psum | solution.py:248
  804.4 62.0 %reduce-scatter.32.cloned.1.call-done = f32[2152,72]{0,1:T(8,128)} async-done(((f32[2152,1152]{0,1:T(8,128)}), f32[2152,72]{0,1:T(8,128)}) %reduce-scatter.32.cloned.1.call-update) | async-done | bytes 619792
  868.3 118.3 %reduce-scatter.28.cloned.1.call-done = f32[72,2152]{1,0:T(8,128)} async-done(((f32[1152,2152]{1,0:T(8,128)}), f32[72,2152]{1,0:T(8,128)}) %reduce-scatter.28.cloned.1.call-update) | async-done | bytes 619792
  988.4 108.9 %reduce-scatter.26.cloned.1.call-done = f32[72,3,576]{2,0,1:T(8,128)} async-done(((f32[1152,3,576]{2,0,1:T(8,128)}), f32[72,3,576]{2,0,1:T(8,128)}) %reduce-scatter.26.cloned.1.call-update) | async-done | bytes 497680 | tf_op jit(solution)/shard_map/reduce_scatter | solution.py:241
  1101.7 40.2 %psum.39 = f32[]{:T(128)} all-reduce(f32[]{:T(128)S(6)} %add.396), channel_id=1, replica_groups=mesh['dp'=16,'tensor'=2] {'dp','tensor'}, use_global_device_ids=true, to_apply=%region_46.47 | all-reduce | flops 1 | bytes 8 | tf_op jit(solution)/shard_map/psum | solution.py:255
  (227 shorter events, 135.8 us)
Async XLA Ops:
  7.2 37.9 %all-gather.11.cloned.1.call-start = ((), (), s32[]{:S(2)}) async-start(), calls=%async_computation.9 | async-start | bytes 2543616 | tf_op jit(solution)/shard_map/all_gather | solution.py:31
  11.2 348.5 %copy-start.31 = (f32[1152]{0:T(1024)}, f32[1152]{0:T(1024)S(1)}, u32[]{:S(2)}) copy-start(f32[1152]{0:T(1024)S(1)} %get-tuple-element.153) | copy-start | bytes 13828
  13.7 86.0 %all-gather.13.cloned.1.call-start = ((), (), s32[]{:S(2)}) async-start(), calls=%async_computation.10 | async-start | bytes 4700160 | tf_op jit(solution)/shard_map/all_gather | solution.py:177
  14.5 125.8 %all-gather.15.cloned.1.call-start = ((), (), s32[]{:S(2)}) async-start(), calls=%async_computation.11 | async-start | bytes 1566720 | tf_op jit(solution)/shard_map/all_gather | solution.py:181
  15.2 155.8 %reduce-scatter.16.cloned.1.call-start = ((), (), s32[]{:S(2)}) async-start(), calls=%async_computation.12 | async-start | bytes 2543616 | tf_op jit(solution)/shard_map/reduce_scatter | solution.py:35
  144.7 84.2 %all-gather.19.cloned.1.call-start = ((), (), s32[]{:S(2)}) async-start(), calls=%async_computation.14 | async-start | bytes 5326848 | tf_op jit(solution)/shard_map/all_gather | solution.py:178
  145.5 139.6 %all-gather.21.cloned.1.call-start = ((), (), s32[]{:S(2)}) async-start(), calls=%async_computation.15 | async-start | bytes 5326848 | tf_op jit(solution)/shard_map/all_gather | solution.py:182
  146.6 167.9 %all-gather.17.cloned.1.call-start = ((), (), s32[]{:S(2)}) async-start(), calls=%async_computation.13 | async-start | bytes 2543616 | tf_op jit(solution)/shard_map/all_gather | solution.py:31
  172.7 141.9 %copy-start.45 = (f32[2152]{0:T(1024)S(1)}, f32[2152]{0:T(1024)}, u32[]{:S(2)}) copy-start(f32[2152]{0:T(1024)} %param.51) | copy-start | bytes 25828
  175.8 180.9 %reduce-scatter.18.cloned.1.call-start = ((), (), s32[]{:S(2)}) async-start(), calls=%async_computation.16 | async-start | bytes 2543616 | tf_op jit(solution)/shard_map/reduce_scatter | solution.py:35
  329.1 60.8 %all-gather.25.cloned.1.call-start = ((), (), s32[]{:S(2)}) async-start(), calls=%async_computation.18 | async-start | bytes 2543616 | tf_op jit(solution)/shard_map/all_gather | solution.py:31
  361.1 93.3 %reduce-scatter.20.cloned.1.call-start = ((), (), s32[]{:S(2)}) async-start(), calls=%async_computation.19 | async-start | bytes 2543616 | tf_op jit(solution)/shard_map/reduce_scatter | solution.py:35
  426.8 61.0 %all-gather.27.cloned.1.call-start = ((), (), s32[]{:S(2)}) async-start(), calls=%async_computation.20 | async-start | bytes 2543616 | tf_op jit(solution)/shard_map/all_gather | solution.py:31
  459.1 58.9 %all-gather.23.cloned.1.call-start = ((), (), s32[]{:S(2)}) async-start(), calls=%async_computation.17 | async-start | bytes 2543616 | tf_op jit(solution)/shard_map/all_gather | solution.py:31
  459.7 106.9 %reduce-scatter.22.cloned.1.call-start = ((), (), s32[]{:S(2)}) async-start(), calls=%async_computation.21 | async-start | bytes 2543616 | tf_op jit(solution)/shard_map/reduce_scatter | solution.py:35
  539.0 60.8 %all-gather.29.cloned.1.call-start = ((), (), s32[]{:S(2)}) async-start(), calls=%async_computation.22 | async-start | bytes 2543616 | tf_op jit(solution)/shard_map/all_gather | solution.py:31
  571.1 183.0 %reduce-scatter.24.cloned.1.call-start = ((), (), s32[]{:S(2)}) async-start(), calls=%async_computation.23 | async-start | bytes 2543616 | tf_op jit(solution)/shard_map/reduce_scatter | solution.py:35
  648.9 153.9 %reduce-scatter.30.cloned.1.call-start = ((), (), s32[]{:S(2)}) async-start(), calls=%async_computation.26 | async-start | bytes 3133440
  654.0 212.5 %reduce-scatter.32.cloned.1.call-start = ((), (), s32[]{:S(2)}) async-start(), calls=%async_computation.27 | async-start | bytes 10653696
  666.4 320.1 %reduce-scatter.28.cloned.1.call-start = ((), (), s32[]{:S(2)}) async-start(), calls=%async_computation.25 | async-start | bytes 10653696
  677.1 420.2 %reduce-scatter.26.cloned.1.call-start = ((), (), s32[]{:S(2)}) async-start(), calls=%async_computation.24 | async-start | bytes 9400320 | tf_op jit(solution)/shard_map/reduce_scatter | solution.py:241
  687.0 67.0 %copy-start.32 = (f32[1152]{0:T(1024)S(1)}, f32[1152]{0:T(1024)}, u32[]{:S(2)}) copy-start(f32[1152]{0:T(1024)} %copy-done.31) | copy-start | bytes 13828
  687.0 67.0 %copy-start.35 = (f32[368]{0:T(512)S(1)}, f32[368]{0:T(512)}, u32[]{:S(2)}) copy-start(f32[368]{0:T(512)} %copy-done.34) | copy-start | bytes 4420
  689.3 68.9 %copy-start.8 = (bf16[1,368,1152]{2,1,0:T(8,128)(2,1)S(1)}, bf16[1,368,1152]{2,1,0:T(8,128)(2,1)}, u32[]{:S(2)}) copy-start(bf16[1,368,1152]{2,1,0:T(8,128)(2,1)} %param.28) | copy-start | bytes 2543620
  758.2 384.4 %copy-start.40 = (f32[2,576]{1,0:T(2,128)S(1)}, f32[2,576]{1,0:T(2,128)}, u32[]{:S(2)}) copy-start(f32[2,576]{1,0:T(2,128)} %param.48) | copy-start | bytes 13828
  758.2 385.7 %copy-start.36 = (f32[2,1152]{1,0:T(2,128)S(1)}, f32[2,1152]{1,0:T(2,128)}, u32[]{:S(2)}) copy-start(f32[2,1152]{1,0:T(2,128)} %param.42) | copy-start | bytes 27652
  758.3 388.4 %copy-start.33 = (f32[4,1152]{1,0:T(4,128)S(1)}, f32[4,1152]{1,0:T(4,128)}, u32[]{:S(2)}) copy-start(f32[4,1152]{1,0:T(4,128)} %param.45) | copy-start | bytes 55300
  758.3 388.4 %copy-start.41 = (f32[4,1152]{1,0:T(4,128)S(1)}, f32[4,1152]{1,0:T(4,128)}, u32[]{:S(2)}) copy-start(f32[4,1152]{1,0:T(4,128)} %param.46) | copy-start | bytes 55300
  758.3 388.4 %copy-start.42 = (f32[4,1152]{1,0:T(4,128)S(1)}, f32[4,1152]{1,0:T(4,128)}, u32[]{:S(2)}) copy-start(f32[4,1152]{1,0:T(4,128)} %param.47) | copy-start | bytes 55300
  760.1 389.5 %copy-start.22 = (f32[72,3,576]{2,0,1:T(8,128)S(1)}, f32[72,3,576]{2,0,1:T(8,128)}, u32[]{:S(2)}) copy-start(f32[72,3,576]{2,0,1:T(8,128)} %param.30) | copy-start | bytes 1492996
  760.1 389.5 %copy-start.29 = (f32[72,3,576]{2,0,1:T(8,128)S(1)}, f32[72,3,576]{2,0,1:T(8,128)}, u32[]{:S(2)}) copy-start(f32[72,3,576]{2,0,1:T(8,128)} %param.31) | copy-start | bytes 1492996
  760.1 389.5 %copy-start.30 = (f32[72,3,576]{2,0,1:T(8,128)S(1)}, f32[72,3,576]{2,0,1:T(8,128)}, u32[]{:S(2)}) copy-start(f32[72,3,576]{2,0,1:T(8,128)} %param.32) | copy-start | bytes 1492996
  (38 other events, 453.3 us)
Sparse Core Ops, SparseCore 0:
  13.8 31.2 all-gather.10
  47.9 51.7 all-gather.12
  102.4 37.8 all-gather.14
  144.8 26.2 reduce-scatter.15
  173.9 54.9 all-gather.18
  231.6 53.4 all-gather.20
  287.3 27.1 all-gather.16
  329.2 27.4 reduce-scatter.17
  361.2 28.5 all-gather.24
  426.9 27.4 reduce-scatter.19
  459.2 28.5 all-gather.26
  489.3 28.5 all-gather.22
  539.1 27.4 reduce-scatter.21
  571.2 28.5 all-gather.28
  649.1 27.3 reduce-scatter.23
  680.8 65.4 reduce-scatter.29
  750.9 115.5 reduce-scatter.31
  871.0 115.4 reduce-scatter.27
  991.2 105.9 reduce-scatter.25
where the time goes:
time: 1170 us; the launch traced here: 1160 us
  waiting for transfers between devices  731 us (62%)
  matrix products  171 us (15%)
  blocking collectives  142 us (12%)
  other arithmetic  90.3 us (8%)
  between operations  22.8 us (2%)
    unnamed x22, waiting for transfers between devices  181 us
    all_gather x6, waiting for transfers between devices, whole_rows(): return lax.all_gather(part, 'tensor', axis=1, tiled=True)  163 us
    reduce_scatter x1, waiting for transfers between devices, on_device(): lax.psum_scatter(joint_weight_grad, 'dp', scatter_dimension=0, tiled=True)  109 us
    reduce_scatter x5, waiting for transfers between devices, share_rows(): lax.psum_scatter(full.astype(jnp.bfloat16), 'tensor', scatter_dimension=1...  107 us
    psum x1, blocking collectives, on_device(): head_sum, hidden_sum = lax.psum((head_grad, hidden_grad), 'dp')  61.9 us
    all_gather x1, waiting for transfers between devices, on_device(): lax.all_gather(reduce_weight.astype(jnp.bfloat16), 'dp', axis=1, tiled=True)  56.3 us
    all_gather x1, waiting for transfers between devices, on_device(): lax.all_gather(joint_weight.astype(jnp.bfloat16), 'dp', axis=0, tiled=True)  54.5 us
    all_gather x1, waiting for transfers between devices, on_device(): lax.all_gather(expand_weight.astype(jnp.bfloat16), 'dp', axis=0, tiled=True)  52.6 us
  transfers between devices with their start and end apart: 19, of which 17 were waited for; matrix products, arithmetic and copies ran while one was open for 9% of the time, Pallas kernels for 0%

commit v1 on v0

--- a/solution.py
+++ b/solution.py
@@ -34,6 +34,12 @@
 def share_rows(full):
     return lax.psum_scatter(
         full.astype(jnp.bfloat16), "tensor", scatter_dimension=1, tiled=True
+    ).astype(jnp.float32)
+
+
+def scatter_sum(part, dim):
+    return lax.psum_scatter(
+        part.astype(jnp.bfloat16), "dp", scatter_dimension=dim, tiled=True
     ).astype(jnp.float32)
 
 
@@ -185,10 +191,6 @@
     small = (norm_gains, shifts, head_bias, hidden_bias)
     layer_rows, saved = forward_pass(tokens, counts, weights, small)
     layer_out = layer_rows.astype(jnp.bfloat16)
-    tokens_held, counts_held, weights_held, anchor = lax.optimization_barrier(
-        (tokens, counts, weights, layer_out)
-    )
-    unused, saved = forward_pass(tokens_held, counts_held, weights_held, small)
     first_back, normed_whole, joint, mixed, logsum, second_back, second_whole, active, gelu_back = (
         saved
     )
@@ -238,12 +240,12 @@
         ]
     )
     joint_sum, expand_sum = (
-        lax.psum_scatter(joint_weight_grad, "dp", scatter_dimension=0, tiled=True),
-        lax.psum_scatter(expand_grad, "dp", scatter_dimension=0, tiled=True),
+        scatter_sum(joint_weight_grad, 0),
+        scatter_sum(expand_grad, 0),
     )
     output_sum, reduce_sum = (
-        lax.psum_scatter(output_grad, "dp", scatter_dimension=1, tiled=True),
-        lax.psum_scatter(reduce_grad, "dp", scatter_dimension=1, tiled=True),
+        scatter_sum(output_grad, 1),
+        scatter_sum(reduce_grad, 1),
     )
     gain_sum, shift_sum = lax.psum((gain_grad, shift_grad), ("dp", "tensor"))
     head_sum, hidden_sum = lax.psum((head_grad, hidden_grad), "dp")

time: 1170 us -> 859 us (0.73)
  waiting for transfers between devices: 731 us -> 442 us
  matrix products: 171 us -> 125 us
  local copies, waits for them, and re-layouts: 5.46 us -> 40.6 us
    reduce_scatter x1 -> x0, waiting for transfers between devices: 109 us -> none  [on_device(): lax.psum_scatter(joint_weight_grad, 'dp', scatter_dimension=0, tiled=True)]
    unnamed x22 -> x20, waiting for transfers between devices: 181 us -> 75.5 us
    all_gather x6 -> x4, waiting for transfers between devices: 163 us -> 107 us  [whole_rows(): return lax.all_gather(part, 'tensor', axis=1, tiled=True)]
    unnamed x102 -> x103, local copies, waits for them, and re-layouts: 4.04 us -> 38.6 us
    dot_general x2 -> x1, matrix products: 17.5 us -> 1.69 us  [attend(): jnp.einsum('hqk,khd->qhd', probs.astype(jnp.bfloat16), values, preferred_...]
    reduce_scatter x5 -> x4, waiting for transfers between devices: 107 us -> 94.5 us  [share_rows(): lax.psum_scatter(full.astype(jnp.bfloat16), 'tensor', scatter_dimension=1...]
  transfers between devices with their start and end apart: 19 -> 16, of which waited for: 17 -> 14; matrix products, arithmetic and copies ran while one was open for 9% -> 22% of each run, Pallas kernels for 0% -> 0%
where the time goes in v1:
time: 859 us; the launch traced here: 854 us
  waiting for transfers between devices  442 us (51%)
  blocking collectives  142 us (17%)
  matrix products  125 us (15%)
  other arithmetic  79.5 us (9%)
  local copies, waits for them, and re-layouts  40.6 us (5%)
  between operations  22.6 us (3%)
    all_gather x4, waiting for transfers between devices, whole_rows(): return lax.all_gather(part, 'tensor', axis=1, tiled=True)  107 us
    reduce_scatter x4, waiting for transfers between devices, share_rows(): lax.psum_scatter(full.astype(jnp.bfloat16), 'tensor', scatter_dimension=1...  94.5 us
    unnamed x20, waiting for transfers between devices  75.5 us
    psum x1, blocking collectives, on_device(): head_sum, hidden_sum = lax.psum((head_grad, hidden_grad), 'dp')  62 us
    all_gather x1, waiting for transfers between devices, on_device(): lax.all_gather(reduce_weight.astype(jnp.bfloat16), 'dp', axis=1, tiled=True)  57.9 us
    all_gather x1, waiting for transfers between devices, on_device(): lax.all_gather(joint_weight.astype(jnp.bfloat16), 'dp', axis=0, tiled=True)  54.5 us
    all_gather x1, waiting for transfers between devices, on_device(): lax.all_gather(expand_weight.astype(jnp.bfloat16), 'dp', axis=0, tiled=True)  51.2 us
    psum x1, blocking collectives, on_device(): gain_sum, shift_sum = lax.psum((gain_grad, shift_grad), ('dp', 'tensor'))  40.8 us
  transfers between devices with their start and end apart: 16, of which 14 were waited for; matrix products, arithmetic and copies ran while one was open for 22% of the time, Pallas kernels for 0%

profile of v1, /device:TPU:0, one launch (start us, length us, event | category | flops | bytes accessed | tf_op | source)
XLA Modules:
  0.0 853.6 jit_solution(2574007469518018370)
XLA Ops:
  17.5 29.0 %all-gather.9.cloned.1.call-done = bf16[1,736,1152]{2,1,0:T(8,128)(2,1)} async-done(((bf16[1,368,1152]{2,1,0:T(8,128)(2,1)}), bf16[1,736,1152]{2,1,0:T(8,128)(2,1)}) %all-gather.9.cloned.1.call-update) | async-done | bytes 1695760 | tf_op jit(solution)/shard_map/all_gather | solution.py:31
  46.5 54.5 %all-gather.11.cloned.1.call-done = bf16[1152,3,576]{2,0,1:T(8,128)(2,1)} async-done(((bf16[72,3,576]{2,0,1:T(8,128)(2,1)}), bf16[1152,3,576]{2,0,1:T(8,128)(2,1)}) %all-gather.11.cloned.1.call-update) | async-done | bytes 3981328 | tf_op jit(solution)/shard_map/all_gather | solution.py:183
  101.0 6.4 add_convert_fusion
  107.7 8.8 %fusion = (f32[8,736]{1,0:T(8,128)S(1)}, f32[8,736,736]{1,2,0:T(8,128)}) fusion(pred[736]{0:T(1024)(128)(4,1)S(1)} %iota_compare_fusion, bf16[736,8,72]{0,2,1:T(8,128)(2,1)S(1)} %bitcast.96, bf16[736,8,72]{0,2,1:T(8,128)(2,1)S(1)} %bitcast.94), kind=kOutput, calls=%fused_computation.5 | convolution fusion | flops 637028608 | bytes 19054304 | tf_op jit(solution)/shard_map/while/body/eval_jaxpr/qhd,khd->hqk/dot_general | solution.py:57
  116.5 10.0 %exponential_reduce_fusion = f32[8,736]{1,0:T(8,128)S(1)} fusion(f32[8,736,736]{1,2,0:T(8,128)} %get-tuple-element.122, f32[8,736]{1,0:T(8,128)S(1)} %get-tuple-element.121, pred[736]{0:T(1024)(128)(4,1)S(1)} %iota_compare_fusion), kind=kLoop, calls=%fused_computation.3 | loop fusion | flops 17328384 | bytes 17382112 | tf_op jit(solution)/shard_map/while/body/eval_jaxpr/reduce_sum | solution.py:68
  126.6 8.2 fusion.1
  146.9 25.5 %reduce-scatter.17.cloned.1.call-done = bf16[1,368,1152]{2,1,0:T(8,128)(2,1)} async-done(((bf16[1,736,1152]{2,1,0:T(8,128)(2,1)}), bf16[1,368,1152]{2,1,0:T(8,128)(2,1)}) %reduce-scatter.17.cloned.1.call-update) | async-done | bytes 847888 | tf_op jit(solution)/shard_map/reduce_scatter | solution.py:35
  179.0 51.2 %all-gather.17.cloned.1.call-done = bf16[1152,2152]{1,0:T(8,128)(2,1)} async-done(((bf16[72,2152]{1,0:T(8,128)(2,1)}), bf16[1152,2152]{1,0:T(8,128)(2,1)}) %all-gather.17.cloned.1.call-update) | async-done | bytes 4958224 | tf_op jit(solution)/shard_map/all_gather | solution.py:184
  230.1 29.2 %all-gather.15.cloned.1.call-done = bf16[1,736,1152]{2,1,0:T(8,128)(2,1)} async-done(((bf16[1,368,1152]{2,1,0:T(8,128)(2,1)}), bf16[1,736,1152]{2,1,0:T(8,128)(2,1)}) %all-gather.15.cloned.1.call-update) | async-done | bytes 1695760 | tf_op jit(solution)/shard_map/all_gather | solution.py:31
  259.4 10.1 %fusion.38 = f32[736,2152]{1,0:T(8,128)} fusion(bf16[1152,2152]{1,0:T(8,128)(2,1)} %all-gather.17.cloned.1.call-done, bf16[1,736,1152]{2,1,0:T(8,128)(2,1)} %all-gather.15.cloned.1.call-done), kind=kOutput, calls=%fused_computation.72 | convolution fusion | flops 3649241088 | bytes 12989440 | tf_op jit(solution)/shard_map/bsd,df->bsf/dot_general | solution.py:117
  269.5 20.1 %all-gather.21.cloned.1.call-done = bf16[1,736,1152]{2,1,0:T(8,128)(2,1)} async-done(((bf16[1,368,1152]{2,1,0:T(8,128)(2,1)}), bf16[1,736,1152]{2,1,0:T(8,128)(2,1)}) %all-gather.21.cloned.1.call-update) | async-done | bytes 1695760 | tf_op jit(solution)/shard_map/all_gather | solution.py:31
  289.6 57.9 %all-gather.19.cloned.1.call-done = bf16[2152,1152]{0,1:T(8,128)(2,1)} async-done(((bf16[2152,72]{0,1:T(8,128)(2,1)}), bf16[2152,1152]{0,1:T(8,128)(2,1)}) %all-gather.19.cloned.1.call-update) | async-done | bytes 4958224 | tf_op jit(solution)/shard_map/all_gather | solution.py:188
  347.5 11.3 %convert_reduce_fusion = (f32[2152]{0:T(1024)S(1)}, bf16[736,2152]{1,0:T(8,128)(2,1)S(1)}) fusion(f32[736,2152]{1,0:T(8,128)} %fusion.38, f32[2152]{0:T(1024)S(1)} %copy-done.46, bf16[2152,1152]{0,1:T(8,128)(2,1)} %all-gather.19.cloned.1.call-done, bf16[1,736,1152]{2,1,0:T(8,128)(2,1)} %all-gather.21.cloned.1.call-done), kind=kOutput, calls=%fused_computation.18 | convolution fusion | flops 3685668096 | bytes 16174400 | tf_op jit(solution)/shard_map/bsd,fd->bsf/dot_general | solution.py:201
  360.5 8.2 fusion.13
  368.9 11.1 %fusion.12 = bf16[1,736,1152]{2,1,0:T(8,128)(2,1)} fusion(bf16[2152,1152]{0,1:T(8,128)(2,1)} %all-gather.19.cloned.1.call-done, f32[736,2152]{1,0:T(8,128)} %fusion.38, f32[2152]{0:T(1024)S(1)} %copy-done.46), kind=kOutput, calls=%fused_computation.31 | convolution fusion | flops 3665927680 | bytes 12998048 | tf_op jit(solution)/shard_map/bsf,fd->bsd/dot_general | solution.py:123
  380.1 14.7 %reduce-scatter.21.cloned.1.call-done = bf16[1,368,1152]{2,1,0:T(8,128)(2,1)} async-done(((bf16[1,736,1152]{2,1,0:T(8,128)(2,1)}), bf16[1,368,1152]{2,1,0:T(8,128)(2,1)}) %reduce-scatter.21.cloned.1.call-update) | async-done | bytes 847888 | tf_op jit(solution)/shard_map/reduce_scatter | solution.py:35
  396.8 27.5 %reduce-scatter.19.cloned.1.call-done = bf16[1,368,1152]{2,1,0:T(8,128)(2,1)} async-done(((bf16[1,736,1152]{2,1,0:T(8,128)(2,1)}), bf16[1,368,1152]{2,1,0:T(8,128)(2,1)}) %reduce-scatter.19.cloned.1.call-update) | async-done | bytes 847888 | tf_op jit(solution)/shard_map/reduce_scatter | solution.py:35
  429.0 28.7 %all-gather.23.cloned.1.call-done = bf16[1,736,1152]{2,1,0:T(8,128)(2,1)} async-done(((bf16[1,368,1152]{2,1,0:T(8,128)(2,1)}), bf16[1,736,1152]{2,1,0:T(8,128)(2,1)}) %all-gather.23.cloned.1.call-update) | async-done | bytes 1695760 | tf_op jit(solution)/shard_map/all_gather | solution.py:31
  462.6 10.1 %convolution_convert_fusion = bf16[2152,1152]{0,1:T(8,128)(2,1)} fusion(bf16[1,736,1152]{2,1,0:T(8,128)(2,1)} %all-gather.21.cloned.1.call-done, f32[736,2152]{1,0:T(8,128)} %fusion.38, f32[2152]{0:T(1024)S(1)} %copy-done.46), kind=kOutput, calls=%fused_computation.6 | convolution fusion | flops 3667558912 | bytes 12998048 | tf_op jit(solution)/shard_map/bsf,bsd->fd/dot_general | solution.py:200
  472.8 9.1 %convolution_convert_fusion.1 = bf16[1152,2152]{1,0:T(8,128)(2,1)} fusion(bf16[736,2152]{1,0:T(8,128)(2,1)} %copy-done.47, bf16[1,736,1152]{2,1,0:T(8,128)(2,1)} %all-gather.15.cloned.1.call-done), kind=kOutput, calls=%fused_computation.7 | convolution fusion | flops 3651720192 | bytes 9821696 | tf_op jit(solution)/shard_map/bsd,bsf->df/dot_general | solution.py:205
  485.2 6.4 convolution_convert_fusion.7
  491.6 13.1 %multiply_reduce_fusion = (f32[8,736]{1,0:T(8,128)S(1)}, f32[8,736,736]{1,2,0:T(8,128)}) fusion(f32[8,736,736]{1,2,0:T(8,128)} %get-tuple-element.122, f32[8,736]{1,0:T(8,128)S(1)} %log_add_fusion, pred[736]{0:T(1024)(128)(4,1)S(1)} %iota_compare_fusion, bf16[736,8,72]{0,2,1:T(8,128)(2,1)S(1)} %bitcast.108, bf16[736,8,72]{0,2,1:T(8,128)(2,1)S(1)} %bitcast.93), kind=kOutput, calls=%fused_computation.1 | convolution fusion | flops 645695744 | bytes 36412128 | tf_op jit(solution)/shard_map/while/body/eval_jaxpr/qhd,khd->hqk/dot_general | solution.py:86
  504.7 13.0 %multiply_convert_fusion = bf16[8,736,736]{1,2,0:T(8,128)(2,1)S(1)} fusion(f32[8,736,736]{1,2,0:T(8,128)} %get-tuple-element.124, f32[8,736,736]{1,2,0:T(8,128)} %get-tuple-element.122, f32[8,736]{1,0:T(8,128)S(1)} %get-tuple-element.123, f32[8,736]{1,0:T(8,128)S(1)} %log_add_fusion, pred[736]{0:T(1024)(128)(4,1)S(1)} %iota_compare_fusion), kind=kLoop, calls=%fused_computation | loop fusion | flops 26001408 | bytes 43383520 | tf_op jit(solution)/shard_map/while/body/eval_jaxpr/convert_element_type | solution.py:88
  529.0 6.3 convolution_convert_fusion.2
  535.3 18.2 %copy.70 = bf16[1152,3,576]{2,1,0:T(4,128)(2,1)} copy(bf16[1152,3,576]{2,0,1:T(8,128)(2,1)S(1)} %convolution_convert_fusion.2) | data formatting | bytes 7962624
  553.5 12.3 %reshape.392 = bf16[1152,1728]{1,0:T(8,128)(2,1)} reshape(bf16[1152,3,576]{2,1,0:T(4,128)(2,1)} %copy.70) | data formatting | bytes 7962624
  568.4 62.0 %all-reduce.4 = (f32[2,576]{1,0:T(2,128)S(1)}, f32[2152]{0:T(1024)S(1)}) all-reduce(f32[2,576]{1,0:T(2,128)S(1)} %convert_reduce_fusion.1, f32[2152]{0:T(1024)S(1)} %get-tuple-element.125), channel_id=1, replica_groups=mesh['dp'=16,'tensor'=2] {'dp'}, use_global_device_ids=true, to_apply=%region_24.25 | all-reduce | flops 3304 | bytes 26432 | tf_op jit(solution)/shard_map/psum | solution.py:251
  636.3 47.3 %reduce-scatter.27.cloned.1.call-done = bf16[72,2152]{1,0:T(8,128)(2,1)} async-done(((bf16[1152,2152]{1,0:T(8,128)(2,1)}), bf16[72,2152]{1,0:T(8,128)(2,1)}) %reduce-scatter.27.cloned.1.call-update) | async-done | bytes 309904
  685.4 26.8 %reduce-scatter.23.cloned.1.call-done = bf16[1,368,1152]{2,1,0:T(8,128)(2,1)} async-done(((bf16[1,736,1152]{2,1,0:T(8,128)(2,1)}), bf16[1,368,1152]{2,1,0:T(8,128)(2,1)}) %reduce-scatter.23.cloned.1.call-update) | async-done | bytes 847888 | tf_op jit(solution)/shard_map/reduce_scatter | solution.py:35
  717.9 40.8 %all-reduce.3 = (f32[2,1152]{1,0:T(2,128)S(1)}, f32[4,1152]{1,0:T(4,128)S(1)}) all-reduce(f32[2,1152]{1,0:T(2,128)S(1)} %pad_maximum_fusion.6, f32[4,1152]{1,0:T(4,128)S(1)} %pad_maximum_fusion.4), channel_id=1, replica_groups=mesh['dp'=16,'tensor'=2] {'dp','tensor'}, use_global_device_ids=true, to_apply=%region_31.32 | all-reduce | flops 6912 | bytes 55296 | tf_op jit(solution)/shard_map/psum | solution.py:250
  761.3 27.2 %reduce-scatter.25.cloned.1.call-done = bf16[72,1728]{1,0:T(8,128)(2,1)} async-done(((bf16[1152,1728]{1,0:T(8,128)(2,1)}), bf16[72,1728]{1,0:T(8,128)(2,1)}) %reduce-scatter.25.cloned.1.call-update) | async-done | bytes 248848
  793.0 39.4 %psum.39 = f32[]{:T(128)} all-reduce(f32[]{:T(128)S(6)} %add.313), channel_id=1, replica_groups=mesh['dp'=16,'tensor'=2] {'dp','tensor'}, use_global_device_ids=true, to_apply=%region_39.40 | all-reduce | flops 1 | bytes 8 | tf_op jit(solution)/shard_map/psum | solution.py:257
  (202 shorter events, 86.2 us)
Async XLA Ops:
  7.2 39.3 %all-gather.9.cloned.1.call-start = ((), (), s32[]{:S(2)}) async-start(), calls=%async_computation.8 | async-start | bytes 2543616 | tf_op jit(solution)/shard_map/all_gather | solution.py:31
  8.7 98.8 %copy-start.35 = (f32[368]{0:T(512)}, f32[368]{0:T(512)S(1)}, u32[]{:S(2)}) copy-start(f32[368]{0:T(512)S(1)} %broadcast_multiply_fusion.1) | copy-start | bytes 4420
  10.8 96.6 %copy-start.38 = (f32[368]{0:T(512)}, f32[368]{0:T(512)S(1)}, u32[]{:S(2)}) copy-start(f32[368]{0:T(512)S(1)} %fusion.61) | copy-start | bytes 4420
  11.6 95.8 %copy-start.30 = (f32[1152]{0:T(1024)}, f32[1152]{0:T(1024)S(1)}, u32[]{:S(2)}) copy-start(f32[1152]{0:T(1024)S(1)} %get-tuple-element.75) | copy-start | bytes 13828
  15.0 86.0 %all-gather.11.cloned.1.call-start = ((), (), s32[]{:S(2)}) async-start(), calls=%async_computation.9 | async-start | bytes 4700160 | tf_op jit(solution)/shard_map/all_gather | solution.py:183
  15.9 125.8 %all-gather.13.cloned.1.call-start = ((), (), s32[]{:S(2)}) async-start(), calls=%async_computation.10 | async-start | bytes 1566720 | tf_op jit(solution)/shard_map/all_gather | solution.py:187
  16.6 155.8 %reduce-scatter.17.cloned.1.call-start = ((), (), s32[]{:S(2)}) async-start(), calls=%async_computation.11 | async-start | bytes 2543616 | tf_op jit(solution)/shard_map/reduce_scatter | solution.py:35
  146.0 84.2 %all-gather.17.cloned.1.call-start = ((), (), s32[]{:S(2)}) async-start(), calls=%async_computation.13 | async-start | bytes 5326848 | tf_op jit(solution)/shard_map/all_gather | solution.py:184
  146.8 112.6 %all-gather.15.cloned.1.call-start = ((), (), s32[]{:S(2)}) async-start(), calls=%async_computation.12 | async-start | bytes 2543616 | tf_op jit(solution)/shard_map/all_gather | solution.py:31
  177.2 112.5 %all-gather.21.cloned.1.call-start = ((), (), s32[]{:S(2)}) async-start(), calls=%async_computation.16 | async-start | bytes 2543616 | tf_op jit(solution)/shard_map/all_gather | solution.py:31
  177.9 169.6 %all-gather.19.cloned.1.call-start = ((), (), s32[]{:S(2)}) async-start(), calls=%async_computation.14 | async-start | bytes 5326848 | tf_op jit(solution)/shard_map/all_gather | solution.py:188
  178.8 168.8 %copy-start.46 = (f32[2152]{0:T(1024)S(1)}, f32[2152]{0:T(1024)}, u32[]{:S(2)}) copy-start(f32[2152]{0:T(1024)} %param.51) | copy-start | bytes 25828
  178.8 216.0 %reduce-scatter.21.cloned.1.call-start = ((), (), s32[]{:S(2)}) async-start(), calls=%async_computation.17 | async-start | bytes 2543616 | tf_op jit(solution)/shard_map/reduce_scatter | solution.py:35
  368.7 55.7 %reduce-scatter.19.cloned.1.call-start = ((), (), s32[]{:S(2)}) async-start(), calls=%async_computation.15 | async-start | bytes 2543616 | tf_op jit(solution)/shard_map/reduce_scatter | solution.py:35
  380.1 77.7 %all-gather.23.cloned.1.call-start = ((), (), s32[]{:S(2)}) async-start(), calls=%async_computation.18 | async-start | bytes 2543616 | tf_op jit(solution)/shard_map/all_gather | solution.py:31
  428.9 204.0 %reduce-scatter.29.cloned.1.call-start = ((), (), s32[]{:S(2)}) async-start(), calls=%async_computation.22 | async-start | bytes 1566720
  462.2 172.3 %reduce-scatter.31.cloned.1.call-start = ((), (), s32[]{:S(2)}) async-start(), calls=%async_computation.23 | async-start | bytes 5326848
  472.7 210.9 %reduce-scatter.27.cloned.1.call-start = ((), (), s32[]{:S(2)}) async-start(), calls=%async_computation.21 | async-start | bytes 5326848
  481.9 230.2 %reduce-scatter.23.cloned.1.call-start = ((), (), s32[]{:S(2)}) async-start(), calls=%async_computation.19 | async-start | bytes 2543616 | tf_op jit(solution)/shard_map/reduce_scatter | solution.py:35
  528.7 259.9 %reduce-scatter.25.cloned.1.call-start = ((), (), s32[]{:S(2)}) async-start(), calls=%async_computation.20 | async-start | bytes 4386816
  565.9 146.2 %copy-start.31 = (f32[1152]{0:T(1024)S(1)}, f32[1152]{0:T(1024)}, u32[]{:S(2)}) copy-start(f32[1152]{0:T(1024)} %copy-done.30) | copy-start | bytes 13828
  565.9 146.2 %copy-start.36 = (f32[368]{0:T(512)S(1)}, f32[368]{0:T(512)}, u32[]{:S(2)}) copy-start(f32[368]{0:T(512)} %copy-done.35) | copy-start | bytes 4420
  568.0 145.9 %copy-start.45 = (f32[368]{0:T(512)S(1)}, f32[368]{0:T(512)}, u32[]{:S(2)}) copy-start(f32[368]{0:T(512)} %copy-done.44) | copy-start | bytes 4420
  568.0 145.9 %copy-start.39 = (f32[368]{0:T(512)S(1)}, f32[368]{0:T(512)}, u32[]{:S(2)}) copy-start(f32[368]{0:T(512)} %copy-done.38) | copy-start | bytes 4420
  568.1 147.9 %copy-start.10 = (bf16[1,368,1152]{2,1,0:T(8,128)(2,1)S(1)}, bf16[1,368,1152]{2,1,0:T(8,128)(2,1)}, u32[]{:S(2)}) copy-start(bf16[1,368,1152]{2,1,0:T(8,128)(2,1)} %param.28) | copy-start | bytes 2543620
  716.0 117.2 %copy-start.41 = (f32[2,576]{1,0:T(2,128)S(1)}, f32[2,576]{1,0:T(2,128)}, u32[]{:S(2)}) copy-start(f32[2,576]{1,0:T(2,128)} %param.48) | copy-start | bytes 13828
  716.0 118.5 %copy-start.37 = (f32[2,1152]{1,0:T(2,128)S(1)}, f32[2,1152]{1,0:T(2,128)}, u32[]{:S(2)}) copy-start(f32[2,1152]{1,0:T(2,128)} %param.42) | copy-start | bytes 27652
  716.0 121.2 %copy-start.34 = (f32[4,1152]{1,0:T(4,128)S(1)}, f32[4,1152]{1,0:T(4,128)}, u32[]{:S(2)}) copy-start(f32[4,1152]{1,0:T(4,128)} %param.45) | copy-start | bytes 55300
  716.1 121.2 %copy-start.42 = (f32[4,1152]{1,0:T(4,128)S(1)}, f32[4,1152]{1,0:T(4,128)}, u32[]{:S(2)}) copy-start(f32[4,1152]{1,0:T(4,128)} %param.46) | copy-start | bytes 55300
  716.1 121.2 %copy-start.43 = (f32[4,1152]{1,0:T(4,128)S(1)}, f32[4,1152]{1,0:T(4,128)}, u32[]{:S(2)}) copy-start(f32[4,1152]{1,0:T(4,128)} %param.47) | copy-start | bytes 55300
  759.4 81.7 %copy-start.32 = (f32[576,72]{0,1:T(8,128)S(1)}, f32[576,72]{0,1:T(8,128)}, u32[]{:S(2)}) copy-start(f32[576,72]{0,1:T(8,128)} %param.34) | copy-start | bytes 497668
  759.4 81.7 %copy-start.33 = (f32[576,72]{0,1:T(8,128)S(1)}, f32[576,72]{0,1:T(8,128)}, u32[]{:S(2)}) copy-start(f32[576,72]{0,1:T(8,128)} %param.35) | copy-start | bytes 497668
  (34 other events, 381.7 us)
Sparse Core Ops, SparseCore 0:
  15.2 31.2 all-gather.8
  49.3 51.7 all-gather.10
  103.8 37.8 all-gather.12
  146.1 26.2 reduce-scatter.16
  175.2 54.8 all-gather.16
  232.2 27.1 all-gather.14
  261.0 28.5 all-gather.20
  292.6 54.9 all-gather.18
  368.8 25.9 reduce-scatter.20
  396.9 27.4 reduce-scatter.18
  429.1 28.5 all-gather.22
  462.3 58.7 reduce-scatter.28
  525.6 77.2 reduce-scatter.30
  606.7 76.8 reduce-scatter.26
  685.8 26.2 reduce-scatter.22
  715.9 72.6 reduce-scatter.24
